TPU v7x, 256 devices: a whole 4x4x8 slice. The times are simulated.
256 devices in a mesh: ctx: 16 (over y, x_lo, core), rep: 8 (over z), head: 2 (over x_hi).
Axes of the slice: x: 4 (x_hi: 2, x_lo: 2; x = x_hi * 2 + x_lo), y: 4, z: 8, core: 2. Of those that a mesh axis runs over, the one named last changes fastest.
Arguments:
- inputs: bfloat16 [8, 8192, 2048], P('rep', 'ctx', 'head'), may hold values from -6 to 6
- queries: bfloat16 [8, 8192, 2048], P('rep', 'ctx', 'head'), may hold values from -6 to 6
- keys: bfloat16 [8, 8192, 2048], P('rep', 'ctx', 'head'), may hold values from -6 to 6
- targets: bfloat16 [8, 8192, 2048], P('rep', 'ctx', 'head'), may hold values from -3 to 3
- value_weight: bfloat16 [8, 2048, 2048], P('rep', None, 'head'), may hold values from -0.125 to 0.125
- anchor: float32 [2048, 2048], P('ctx', 'head'), may hold values from -0.125 to 0.125
- momentum: float32 [2048, 2048], P('ctx', 'head'), may hold values from -6 to 6
Outputs:
- anchor_next: float32 [8, 2048, 2048], P('rep', 'ctx', 'head')
- momentum_next: float32 [8, 2048, 2048], P('rep', 'ctx', 'head')
All inputs are finite; a program needn't handle non-finite values.
Results may differ from a plain program's by a relative error of at most 0.02.
Values may be sent and summed in bfloat16 or wider, within the bound.
A program may use at most 64 MiB of HBM per device.

v0:
```python
import math
import jax
import jax.numpy as jnp
from jax import lax
from jax.sharding import PartitionSpec as P

HEAD_DIM = 128
inner_rate = 0.05
slow_decay = 0.5
outer_rate = 1.0


def carried_in(shard, axis, join, neutral, backward):
    count = lax.axis_size(axis)
    place = lax.axis_index(axis)
    ahead = count - 1 - place if backward else place
    gathered = lax.all_gather(shard.astype(jnp.bfloat16), axis)
    state = jnp.zeros_like(shard) + jnp.asarray(neutral, shard.dtype)

    def one(turn, state):
        source = count - 1 - turn if backward else turn
        return join(state, lax.dynamic_index_in_dim(gathered, source, 0, False).astype(shard.dtype))

    return lax.fori_loop(0, ahead, one, state)


def from_partner(block, axis, apart):
    count = lax.axis_size(axis)
    route = []
    for low in range(count):
        high = low | 1 << apart
        if high != low and high < count:
            route += [(low, high), (high, low)]
    return lax.ppermute(block, axis, route)


def add_states(earlier, later):
    return earlier + later


def carried(local_state, forward):
    empty = jnp.zeros_like(local_state)
    if forward:
        return carried_in(local_state, "ctx", add_states, empty, False)
    return carried_in(local_state, "ctx", add_states, empty, True)


def mix_total(delta):
    for bit_number in range(2):
        delta = (
            delta + from_partner(delta.astype(jnp.bfloat16), "rep", bit_number).astype(delta.dtype)
        ) * 0.5
    return delta


def mix_rows(delta):
    return mix_total(delta)


def local(inputs, queries, keys, targets, value_weight, anchor, momentum):
    n_blocks = lax.axis_size("ctx")
    tokens_here = queries.shape[1]
    local_width = queries.shape[2]
    heads_here = local_width // HEAD_DIM
    sequence = tokens_here * n_blocks
    attn_scale = 1.0 / math.sqrt(HEAD_DIM * sequence)
    loss_scale = 1.0 / math.sqrt(sequence)
    weights_local = value_weight[0]
    model_width = weights_local.shape[0]
    share_rows = model_width // n_blocks
    first_row = lax.axis_index("ctx") * share_rows
    weight_rows = lax.dynamic_slice_in_dim(weights_local, first_row, share_rows, 0).astype(
        jnp.float32
    )
    drift = (anchor - weight_rows) / inner_rate
    features = lax.all_gather(inputs, "head", axis=2, tiled=True)[0]
    values = jnp.dot(features, weights_local, preferred_element_type=jnp.float32).astype(
        jnp.bfloat16
    )
    query_heads = queries[0].reshape(tokens_here, heads_here, HEAD_DIM)
    key_heads = keys[0].reshape(tokens_here, heads_here, HEAD_DIM)
    value_heads = values.reshape(tokens_here, heads_here, HEAD_DIM)
    target_heads = targets[0].reshape(tokens_here, heads_here, HEAD_DIM)
    scores = jnp.einsum("thd,shd->hts", query_heads, key_heads, preferred_element_type=jnp.float32)
    causal = jnp.arange(tokens_here)[:, None] >= jnp.arange(tokens_here)[None, :]
    weighted = jnp.where(causal[None], scores, 0.0).astype(jnp.bfloat16)
    local_state = jnp.einsum(
        "shd,she->hde", key_heads, value_heads, preferred_element_type=jnp.float32
    )
    prefix_state = carried(local_state, True)
    outputs = attn_scale * (
        jnp.einsum("hts,she->the", weighted, value_heads, preferred_element_type=jnp.float32)
        + jnp.einsum(
            "thd,hde->the",
            query_heads,
            prefix_state.astype(jnp.bfloat16),
            preferred_element_type=jnp.float32,
        )
    )
    grad_out = (loss_scale * (outputs - target_heads.astype(jnp.float32))).astype(jnp.bfloat16)
    back_local = jnp.einsum(
        "thd,the->hde", query_heads, grad_out, preferred_element_type=jnp.float32
    )
    suffix_state = carried(back_local, False)
    grad_values = attn_scale * (
        jnp.einsum("hts,the->she", weighted, grad_out, preferred_element_type=jnp.float32)
        + jnp.einsum(
            "shd,hde->she",
            key_heads,
            suffix_state.astype(jnp.bfloat16),
            preferred_element_type=jnp.float32,
        )
    )
    grad_values = grad_values.astype(jnp.bfloat16).reshape(tokens_here, local_width)
    gradient = lax.psum_scatter(
        lax.dot_general(
            features, grad_values, (((0,), (0,)), ((), ())), preferred_element_type=jnp.float32
        ).astype(jnp.bfloat16),
        "ctx",
        scatter_dimension=0,
        tiled=True,
    ).astype(jnp.float32)
    mixed = mix_rows(drift + gradient)
    momentum_next = slow_decay * momentum + mixed
    anchor_next = anchor - outer_rate * inner_rate * momentum_next
    return (anchor_next[None], momentum_next[None])


def solution(mesh):
    placed = (
        P("rep", "ctx", "head"),
        P("rep", "ctx", "head"),
        P("rep", "ctx", "head"),
        P("rep", "ctx", "head"),
        P("rep", None, "head"),
        P("ctx", "head"),
        P("ctx", "head"),
    )
    return jax.shard_map(
        local,
        mesh=mesh,
        in_specs=placed,
        out_specs=(P("rep", "ctx", "head"), P("rep", "ctx", "head")),
        check_vma=False,
    )
```

profile of v0, /device:TPU:27, one launch (start us, length us, event | category | flops | bytes accessed | tf_op | source)
XLA Modules:
  0.0 289.3 jit_solution(1893113426766698581)
XLA Ops:
  7.2 0.0 all-gather.6.cloned.1.call-start
  7.2 0.7 all-gather.6.cloned.1.call-update
  7.9 0.0 all-gather.8.cloned.1.call-start
  7.9 1.5 copy.54
  9.4 0.0 copy-start.2
  9.4 41.6 %all-gather.6.cloned.1.call-done = bf16[1,512,2048]{2,1,0:T(8,128)(2,1)} async-done(((bf16[1,512,1024]{2,1,0:T(8,128)(2,1)}), bf16[1,512,2048]{2,1,0:T(8,128)(2,1)}) %all-gather.6.cloned.1.call-update) | async-done | bytes 2097168 | tf_op jit(solution)/shard_map/all_gather | solution.py:76
  51.1 5.2 %fusion.6 = bf16[512,1024]{1,0:T(8,128)(2,1)S(1)} fusion(bf16[1,2048,1024]{2,1,0:T(8,128)(2,1)} %param.15, bf16[1,512,2048]{2,1,0:T(8,128)(2,1)} %all-gather.6.cloned.1.call-done), kind=kOutput, calls=%fused_computation.12 | convolution fusion | flops 2148007936 | bytes 7340032 | tf_op jit(solution)/shard_map/dot_general | solution.py:77
  56.2 0.5 copy.51
  56.8 0.5 fusion.11
  57.3 0.9 copy.35
  58.1 0.0 all-gather.8.cloned.1.call-update
  58.1 0.0 all-gather.10.cloned.1.call-start
  58.2 1.5 copy.53
  59.7 0.0 copy-start.3
  59.7 3.0 %copy.38 = f32[1,512,1024]{1,2,0:T(8,128)} copy(bf16[1,512,1024]{2,1,0:T(8,128)(2,1)} %param.14) | data formatting | bytes 3145728 | tf_op jit(solution)/shard_map/convert_element_type | solution.py:100
  62.7 0.1 iota_compare_fusion
  62.8 1.4 select_convert_fusion
  64.2 1.9 copy-done
  66.1 1.5 fusion.25
  67.6 29.8 %all-gather.8.cloned.1.call-done = bf16[128,128,128]{2,1,0:T(8,128)(2,1)} async-done(((bf16[8,128,128]{2,1,0:T(8,128)(2,1)}), bf16[128,128,128]{2,1,0:T(8,128)(2,1)}) %all-gather.8.cloned.1.call-update) | async-done | bytes 4194320 | tf_op jit(solution)/shard_map/all_gather | solution.py:17
  97.4 16.5 %while.22 = (s32[]{:T(128)}, f32[8,128,128]{2,1,0:T(8,128)S(1)}, s32[]{:T(128)}, bf16[16,8,128,128]{3,2,1,0:T(8,128)(2,1)}, s32[]{:T(128)}, /*index=5*/s32[]{:T(128)}, s32[]{:T(128)}) while((s32[]{:T(128)}, f32[8,128,128]{2,1,0:T(8,128)S(1)}, s32[]{:T(128)}, bf16[16,8,128,128]{3,2,1,0:T(8,128)(2,1)}, s32[]{:T(128)}, /*index=5*/s32[]{:T(128)}, ...), condition=%wide.region_1.2_spmd, body=%wide.region_0.1_spmd.sunk | while | flops 262149 | bytes 1310835 | solution.py:24
  97.4 1.1 convert_add_fusion.4
  98.5 1.1 convert_add_fusion.4
  99.6 1.1 convert_add_fusion.4
  100.7 1.1 convert_add_fusion.4
  101.8 1.1 convert_add_fusion.4
  102.9 1.1 convert_add_fusion.4
  104.0 1.1 convert_add_fusion.4
  105.1 1.1 convert_add_fusion.4
  106.2 1.1 convert_add_fusion.4
  107.3 1.1 convert_add_fusion.4
  108.4 1.1 convert_add_fusion.4
  109.5 1.1 convert_add_fusion.4
  110.6 1.1 convert_add_fusion.4
  111.7 1.1 convert_add_fusion.4
  112.8 1.1 convert_add_fusion.4
  113.9 2.6 fusion.3
  116.5 1.0 copy-done.1
  117.5 0.5 fusion.12
  118.0 0.9 copy.40
  118.8 0.0 all-gather.10.cloned.1.call-update
  118.9 0.0 reduce-scatter.4.cloned.1.call-start
  118.9 3.2 %fusion.26 = f32[8,128,512]{2,1,0:T(8,128)S(1)} fusion(bf16[512,8,128]{0,2,1:T(8,128)(2,1)} %copy-done.1, bf16[8,512,512]{2,1,0:T(8,128)(2,1)} %copy-done), kind=kOutput, calls=%fused_computation.37 | convolution fusion | flops 536870912 | bytes 7340032 | tf_op jit(solution)/shard_map/hts,the->she/dot_general | solution.py:106
  122.1 35.7 %all-gather.10.cloned.1.call-done = bf16[128,128,128]{2,1,0:T(8,128)(2,1)} async-done(((bf16[8,128,128]{2,1,0:T(8,128)(2,1)}), bf16[128,128,128]{2,1,0:T(8,128)(2,1)}) %all-gather.10.cloned.1.call-update) | async-done | bytes 4194320 | tf_op jit(solution)/shard_map/all_gather | solution.py:17
  157.9 1.9 multiply_convert_fusion
  159.8 4.3 %convert_bitcast_fusion = bf16[2048,1024]{0,1:T(8,128)(2,1)} fusion(bf16[512,1024]{0,1:T(8,128)(2,1)S(1)} %bitcast.81, bf16[1,512,2048]{2,1,0:T(8,128)(2,1)S(1)} %copy-done.7), kind=kOutput, calls=%fused_computation.5 | convolution fusion | flops 2149580800 | bytes 7340032 | tf_op jit(solution)/shard_map/dot_general | solution.py:116
  164.2 6.4 %copy.49 = bf16[2048,1024]{1,0:T(8,128)(2,1)} copy(bf16[2048,1024]{0,1:T(8,128)(2,1)} %convert_bitcast_fusion) | data formatting | bytes 8388608
  170.6 0.0 reduce-scatter.4.cloned.1.call-update
  170.6 1.0 constant_dynamic-slice_fusion
  171.6 0.2 copy.52
  171.8 0.0 copy-start.6
  171.8 0.2 copy.44
  172.0 86.7 %reduce-scatter.4.cloned.1.call-done = bf16[128,1024]{1,0:T(8,128)(2,1)} async-done(((bf16[2048,1024]{1,0:T(8,128)(2,1)}), bf16[128,1024]{1,0:T(8,128)(2,1)}) %reduce-scatter.4.cloned.1.call-update) | async-done | bytes 262160
  258.7 1.1 copy.50
  259.8 0.1 fusion.24
  259.9 1.4 collective-permute-start
  261.3 5.0 %collective-permute-done = bf16[128,1024]{0,1:T(8,128)(2,1)S(1)} collective-permute-done((bf16[128,1024]{0,1:T(8,128)(2,1)S(1)}, bf16[128,1024]{0,1:T(8,128)(2,1)S(1)}, u32[]{:S(2)}, u32[]{:S(2)}) %collective-permute-start) | collective-permute-done | bytes 262176 | tf_op jit(solution)/shard_map/ppermute | solution.py:34
  266.3 0.2 fusion.21
  266.5 2.4 collective-permute-start.1
  268.9 0.2 copy.43
  269.1 11.4 %collective-permute-done.1 = bf16[128,1024]{0,1:T(8,128)(2,1)S(1)} collective-permute-done((bf16[128,1024]{0,1:T(8,128)(2,1)S(1)}, bf16[128,1024]{0,1:T(8,128)(2,1)S(1)}, u32[]{:S(2)}, u32[]{:S(2)}) %collective-permute-start.1) | collective-permute-done | bytes 262176 | tf_op jit(solution)/shard_map/ppermute | solution.py:34
  280.5 0.2 multiply_bitcast_fusion
  280.8 1.0 copy.45
  281.8 1.0 copy.46
  (14 shorter events, 0.1 us)
Async XLA Ops:
  7.2 43.9 %all-gather.6.cloned.1.call-start = ((), (), s32[]{:S(2)}) async-start(), calls=%async_computation.1 | async-start | bytes 3145728 | tf_op jit(solution)/shard_map/all_gather | solution.py:76
  7.9 89.5 %all-gather.8.cloned.1.call-start = ((), (), s32[]{:S(2)}) async-start(), calls=%async_computation.2 | async-start | bytes 4456448 | tf_op jit(solution)/shard_map/all_gather | solution.py:17
  9.4 53.3 %copy-start.2 = (bf16[64,8,8,128]{3,2,1,0:T(8,128)(2,1)}, bf16[64,8,8,128]{3,2,1,0:T(8,128)(2,1)S(1)}, u32[]{:S(2)}) copy-start(bf16[64,8,8,128]{3,2,1,0:T(8,128)(2,1)S(1)} %copy.54) | copy-start | bytes 3145732
  58.1 99.7 %all-gather.10.cloned.1.call-start = ((), (), s32[]{:S(2)}) async-start(), calls=%async_computation.3 | async-start | bytes 4456448 | tf_op jit(solution)/shard_map/all_gather | solution.py:17
  59.7 3.1 %copy-start.3 = (bf16[64,8,8,128]{3,2,1,0:T(8,128)(2,1)}, bf16[64,8,8,128]{3,2,1,0:T(8,128)(2,1)S(1)}, u32[]{:S(2)}) copy-start(bf16[64,8,8,128]{3,2,1,0:T(8,128)(2,1)S(1)} %copy.53) | copy-start | bytes 3145732
  64.2 1.9 copy-start
  113.9 3.6 %copy-start.4 = (bf16[64,8,8,128]{3,2,1,0:T(8,128)(2,1)S(1)}, bf16[64,8,8,128]{3,2,1,0:T(8,128)(2,1)}, u32[]{:S(2)}) copy-start(bf16[64,8,8,128]{3,2,1,0:T(8,128)(2,1)} %copy-done.3) | copy-start | bytes 3145732
  116.5 1.0 copy-start.1
  118.9 139.8 %reduce-scatter.4.cloned.1.call-start = ((), (), s32[]{:S(2)}) async-start(), calls=%async_computation.4 | async-start | bytes 4456448
  157.9 1.9 copy-start.7
  170.6 1.2 copy-start.5
  171.8 97.1 %copy-start.6 = (f32[128,1024]{1,0:T(8,128)S(1)}, f32[128,1024]{1,0:T(8,128)}, u32[]{:S(2)}) copy-start(f32[128,1024]{1,0:T(8,128)} %param.17) | copy-start | bytes 1572868
  259.9 6.4 %collective-permute-start = (bf16[128,1024]{0,1:T(8,128)(2,1)S(1)}, bf16[128,1024]{0,1:T(8,128)(2,1)S(1)}, u32[]{:S(2)}, u32[]{:S(2)}) collective-permute-start(bf16[128,1024]{0,1:T(8,128)(2,1)S(1)} %fusion.24), channel_id=1, source_target_pairs={{0,2},{2,0},{4,6},{6,4},{8,10},{10,8},{12,14},{14,12},{1,3},{3,1},... | collective-permute-start | bytes 786440 | tf_op jit(solution)/shard_map/ppermute | solution.py:34
  266.5 14.0 %collective-permute-start.1 = (bf16[128,1024]{0,1:T(8,128)(2,1)S(1)}, bf16[128,1024]{0,1:T(8,128)(2,1)S(1)}, u32[]{:S(2)}, u32[]{:S(2)}) collective-permute-start(bf16[128,1024]{0,1:T(8,128)(2,1)S(1)} %fusion.21), channel_id=1, source_target_pairs={{0,4},{4,0},{2,6},{6,2},{8,12},{12,8},{10,14},{14,10},{1,5},{5,1},... | collective-permute-start | bytes 786440 | tf_op jit(solution)/shard_map/ppermute | solution.py:34
Sparse Core Ops, SparseCore 0:
  9.8 41.2 all-gather.5
  58.3 39.0 all-gather.7
  119.0 38.7 all-gather.9
  170.7 87.9 reduce-scatter.3
where the time goes:
time: 290 us; the launch traced here: 289 us
  waiting for transfers between devices  211 us (73%)
  local copies, waits for them, and re-layouts  22.3 us (8%)
  matrix products  21 us (7%)
  other arithmetic  16.6 us (6%)
  between operations  14 us (5%)
  starting transfers between devices  3.93 us (1%)
    unnamed x5, waiting for transfers between devices  87.4 us
    all_gather x2, waiting for transfers between devices, carried_in(): gathered = lax.all_gather(shard.astype(jnp.bfloat16), axis)  65.5 us
    all_gather x1, waiting for transfers between devices, local(): features = lax.all_gather(inputs, 'head', axis=2, tiled=True)[0]  41.6 us
    ppermute x2, waiting for transfers between devices, from_partner(): return lax.ppermute(block, axis, route)  16.4 us
    add x15, other arithmetic, add_states(): return earlier + later  16 us
    unnamed x25, local copies, waits for them, and re-layouts  16 us
  transfers between devices with their start and end apart: 6, of which 6 were waited for; matrix products, arithmetic and copies ran while one was open for 5% of the time, Pallas kernels for 0%

commit v1 on v0

--- a/solution.py
+++ b/solution.py
@@ -8,6 +8,11 @@
 inner_rate = 0.05
 slow_decay = 0.5
 outer_rate = 1.0
+
+
+def all_by_exchange(x, axis, dim):
+    stack = jnp.stack([x] * lax.axis_size(axis))
+    return jnp.concatenate(lax.all_to_all(stack, axis, 0, 0), axis=dim)
 
 
 def carried_in(shard, axis, join, neutral, backward):
@@ -73,7 +78,7 @@
         jnp.float32
     )
     drift = (anchor - weight_rows) / inner_rate
-    features = lax.all_gather(inputs, "head", axis=2, tiled=True)[0]
+    features = all_by_exchange(inputs, "head", 2)[0]
     values = jnp.dot(features, weights_local, preferred_element_type=jnp.float32).astype(
         jnp.bfloat16
     )

time: 290 us -> 275 us (0.948)
  waiting for transfers between devices: 211 us -> 196 us
  local copies, waits for them, and re-layouts: 22.3 us -> 15 us
  starting transfers between devices: 3.93 us -> 7.6 us
  other arithmetic: 16.6 us -> 20 us
    reduce_scatter x0 -> x1, waiting for transfers between devices: none -> 88 us  [local(): lax.psum_scatter(lax.dot_general(features, grad_values, (((0,), (0,)), ((...]
    unnamed x5 -> x3, waiting for transfers between devices: 87.4 us -> 0.05 us
    all_gather x1 -> x0, waiting for transfers between devices: 41.6 us -> none  [local(): features = lax.all_gather(inputs, 'head', axis=2, tiled=True)[0]]
    all_to_all x0 -> x1, waiting for transfers between devices: none -> 24.2 us  [all_by_exchange(): return jnp.concatenate(lax.all_to_all(stack, axis, 0, 0), axis=dim)]
    unnamed x25 -> x21, local copies, waits for them, and re-layouts: 16 us -> 8.8 us
    all_to_all x0 -> x1, starting transfers between devices: none -> 3.76 us  [all_by_exchange(): return jnp.concatenate(lax.all_to_all(stack, axis, 0, 0), axis=dim)]
  transfers between devices with their start and end apart: 6 -> 6, of which waited for: 6 -> 6; matrix products, arithmetic and copies ran while one was open for 5% -> 4% of each run, Pallas kernels for 0% -> 0%
where the time goes in v1:
time: 275 us; the launch traced here: 274 us
  waiting for transfers between devices  196 us (71%)
  matrix products  21.4 us (8%)
  other arithmetic  20 us (7%)
  local copies, waits for them, and re-layouts  15 us (5%)
  between operations  14 us (5%)
  starting transfers between devices  7.6 us (3%)
    reduce_scatter x1, waiting for transfers between devices, local(): lax.psum_scatter(lax.dot_general(features, grad_values, (((0,), (0,)), ((...  88 us
    all_gather x2, waiting for transfers between devices, carried_in(): gathered = lax.all_gather(shard.astype(jnp.bfloat16), axis)  67 us
    all_to_all x1, waiting for transfers between devices, all_by_exchange(): return jnp.concatenate(lax.all_to_all(stack, axis, 0, 0), axis=dim)  24.2 us
    ppermute x2, waiting for transfers between devices, from_partner(): return lax.ppermute(block, axis, route)  16.9 us
    add x15, other arithmetic, add_states(): return earlier + later  16 us
    unnamed x21, local copies, waits for them, and re-layouts  8.8 us
    dot_general x1, matrix products, local(): jnp.dot(features, weights_local, preferred_element_type=jnp.float32)  5.51 us
  transfers between devices with their start and end apart: 6, of which 6 were waited for; matrix products, arithmetic and copies ran while one was open for 4% of the time, Pallas kernels for 0%

profile of v1, /device:TPU:27, one launch (start us, length us, event | category | flops | bytes accessed | tf_op | source)
XLA Modules:
  0.0 274.4 jit_solution(2002932009475033674)
XLA Ops:
  7.2 1.5 copy.36
  8.7 1.5 pad_maximum_fusion
  10.2 3.8 %all-to-all-start = ((bf16[2,1,512,1024]{2,3,1,0:T(8,128)(2,1)}), bf16[2,1,512,1024]{2,3,1,0:T(8,128)(2,1)S(1)}, u32[]{:S(2)}, u32[]{:S(2)}) async-start(bf16[2,1,512,1024]{2,3,1,0:T(8,128)(2,1)} %pad_maximum_fusion), calls=%async_computation | async-start | bytes 4194304 | tf_op jit(solution)/shard_map/all_to_all | solution.py:15
  13.9 0.0 all-gather.5.cloned.1.call-start
  14.0 1.5 copy.55
  15.5 0.0 copy-start.2
  15.5 24.2 %all-to-all-done = bf16[2,1,512,1024]{2,3,1,0:T(8,128)(2,1)S(1)} async-done(((bf16[2,1,512,1024]{2,3,1,0:T(8,128)(2,1)}), bf16[2,1,512,1024]{2,3,1,0:T(8,128)(2,1)S(1)}, u32[]{:S(2)}, u32[]{:S(2)}) %all-to-all-start) | async-done | bytes 2097184 | tf_op jit(solution)/shard_map/all_to_all | solution.py:15
  39.7 1.4 copy-done.5
  41.1 5.5 %fusion.4 = bf16[512,1024]{1,0:T(8,128)(2,1)} fusion(bf16[512,2048]{0,1:T(8,128)(2,1)S(1)} %bitcast.71, bf16[1,2048,1024]{2,1,0:T(8,128)(2,1)} %param.15), kind=kOutput, calls=%fused_computation.11 | convolution fusion | flops 2148007936 | bytes 7340032 | tf_op jit(solution)/shard_map/dot_general | solution.py:82
  46.6 1.5 copy.53
  48.1 0.5 fusion.7
  48.6 0.9 copy.43
  49.4 0.0 all-gather.5.cloned.1.call-update
  49.4 0.0 all-gather.7.cloned.1.call-start
  49.5 1.5 copy.54
  51.0 3.0 %copy.46 = f32[1,512,1024]{1,2,0:T(8,128)} copy(bf16[1,512,1024]{2,1,0:T(8,128)(2,1)} %param.14) | data formatting | bytes 3145728 | tf_op jit(solution)/shard_map/convert_element_type | solution.py:105
  54.0 0.1 iota_compare_fusion
  54.1 0.0 copy-done.2
  54.1 0.0 copy-done.3
  54.1 1.4 select_convert_fusion
  55.4 0.0 copy-start
  55.5 1.9 copy-done
  57.4 1.5 fusion.22
  58.9 31.3 %all-gather.5.cloned.1.call-done = bf16[128,128,128]{2,1,0:T(8,128)(2,1)} async-done(((bf16[8,128,128]{2,1,0:T(8,128)(2,1)}), bf16[128,128,128]{2,1,0:T(8,128)(2,1)}) %all-gather.5.cloned.1.call-update) | async-done | bytes 4194320 | tf_op jit(solution)/shard_map/all_gather | solution.py:22
  90.2 16.4 %while.22 = (s32[]{:T(128)}, f32[8,128,128]{2,1,0:T(8,128)S(1)}, s32[]{:T(128)}, bf16[16,8,128,128]{3,2,1,0:T(8,128)(2,1)}, s32[]{:T(128)}, /*index=5*/s32[]{:T(128)}, s32[]{:T(128)}) while((s32[]{:T(128)}, f32[8,128,128]{2,1,0:T(8,128)S(1)}, s32[]{:T(128)}, bf16[16,8,128,128]{3,2,1,0:T(8,128)(2,1)}, s32[]{:T(128)}, /*index=5*/s32[]{:T(128)}, ...), condition=%wide.region_1.2_spmd, body=%wide.region_0.1_spmd.sunk | while | flops 262149 | bytes 1310843 | solution.py:29
  90.2 1.1 convert_add_fusion.4
  91.3 1.1 convert_add_fusion.4
  92.4 1.1 convert_add_fusion.4
  93.5 1.1 convert_add_fusion.4
  94.6 1.1 convert_add_fusion.4
  95.7 1.1 convert_add_fusion.4
  96.8 1.1 convert_add_fusion.4
  97.9 1.1 convert_add_fusion.4
  98.9 1.1 convert_add_fusion.4
  100.0 1.1 convert_add_fusion.4
  101.1 1.1 convert_add_fusion.4
  102.2 1.1 convert_add_fusion.4
  103.3 1.1 convert_add_fusion.4
  104.4 1.1 convert_add_fusion.4
  105.5 1.1 convert_add_fusion.4
  106.6 2.6 fusion.3
  109.2 1.0 copy-done.1
  110.2 0.0 copy-done.4
  110.2 0.5 fusion.8
  110.7 0.9 copy.48
  111.5 0.0 all-gather.7.cloned.1.call-update
  111.6 0.0 reduce-scatter.2.cloned.1.call-start
  111.6 3.2 %fusion.23 = f32[8,128,512]{2,1,0:T(8,128)S(1)} fusion(bf16[512,8,128]{0,2,1:T(8,128)(2,1)} %copy-done.1, bf16[8,512,512]{2,1,0:T(8,128)(2,1)} %copy-done), kind=kOutput, calls=%fused_computation.35 | convolution fusion | flops 536870912 | bytes 7340032 | tf_op jit(solution)/shard_map/hts,the->she/dot_general | solution.py:111
  114.8 35.7 %all-gather.7.cloned.1.call-done = bf16[128,128,128]{2,1,0:T(8,128)(2,1)} async-done(((bf16[8,128,128]{2,1,0:T(8,128)(2,1)}), bf16[128,128,128]{2,1,0:T(8,128)(2,1)}) %all-gather.7.cloned.1.call-update) | async-done | bytes 4194320 | tf_op jit(solution)/shard_map/all_gather | solution.py:22
  150.6 0.0 copy-start.6
  150.6 1.9 multiply_convert_fusion
  152.5 0.0 copy-done.6
  152.5 4.3 %convolution_convert_fusion = bf16[2048,1024]{1,0:T(8,128)(2,1)} fusion(bf16[512,2048]{0,1:T(8,128)(2,1)S(1)} %bitcast.72, bf16[512,1024]{0,1:T(8,128)(2,1)S(1)} %bitcast.75), kind=kOutput, calls=%fused_computation.5 | convolution fusion | flops 2149580800 | bytes 7340032 | tf_op jit(solution)/shard_map/dot_general | solution.py:121
  156.8 0.0 reduce-scatter.2.cloned.1.call-update
  156.9 0.0 copy-start.8
  156.9 88.0 %reduce-scatter.2.cloned.1.call-done = bf16[128,1024]{1,0:T(8,128)(2,1)} async-done(((bf16[2048,1024]{1,0:T(8,128)(2,1)}), bf16[128,1024]{1,0:T(8,128)(2,1)}) %reduce-scatter.2.cloned.1.call-update) | async-done | bytes 262160 | tf_op jit(solution)/shard_map/reduce_scatter | solution.py:120
  244.9 1.1 fusion.20
  246.0 1.5 collective-permute-start
  247.6 4.9 %collective-permute-done = bf16[128,1024]{1,0:T(8,128)(2,1)S(1)} collective-permute-done((bf16[128,1024]{1,0:T(8,128)(2,1)S(1)}, bf16[128,1024]{1,0:T(8,128)(2,1)S(1)}, u32[]{:S(2)}, u32[]{:S(2)}) %collective-permute-start) | collective-permute-done | bytes 262176 | tf_op jit(solution)/shard_map/ppermute | solution.py:39
  252.5 0.1 fusion.17
  252.6 2.2 collective-permute-start.1
  254.7 11.9 %collective-permute-done.1 = bf16[128,1024]{1,0:T(8,128)(2,1)S(1)} collective-permute-done((bf16[128,1024]{1,0:T(8,128)(2,1)S(1)}, bf16[128,1024]{1,0:T(8,128)(2,1)S(1)}, u32[]{:S(2)}, u32[]{:S(2)}) %collective-permute-start.1) | collective-permute-done | bytes 262176 | tf_op jit(solution)/shard_map/ppermute | solution.py:39
  266.7 0.0 copy-done.8
  266.7 1.1 multiply_bitcast_fusion
  (9 shorter events, 0.1 us)
Async XLA Ops:
  10.2 29.5 %all-to-all-start = ((bf16[2,1,512,1024]{2,3,1,0:T(8,128)(2,1)}), bf16[2,1,512,1024]{2,3,1,0:T(8,128)(2,1)S(1)}, u32[]{:S(2)}, u32[]{:S(2)}) async-start(bf16[2,1,512,1024]{2,3,1,0:T(8,128)(2,1)} %pad_maximum_fusion), calls=%async_computation | async-start | bytes 4194304 | tf_op jit(solution)/shard_map/all_to_all | solution.py:15
  13.9 76.2 %all-gather.5.cloned.1.call-start = ((), (), s32[]{:S(2)}) async-start(), calls=%async_computation.3 | async-start | bytes 4456448 | tf_op jit(solution)/shard_map/all_gather | solution.py:22
  15.5 38.6 %copy-start.2 = (bf16[64,8,8,128]{3,2,1,0:T(8,128)(2,1)}, bf16[64,8,8,128]{3,2,1,0:T(8,128)(2,1)S(1)}, u32[]{:S(2)}) copy-start(bf16[64,8,8,128]{3,2,1,0:T(8,128)(2,1)S(1)} %copy.55) | copy-start | bytes 3145732
  39.7 1.4 copy-start.5
  49.4 101.1 %all-gather.7.cloned.1.call-start = ((), (), s32[]{:S(2)}) async-start(), calls=%async_computation.4 | async-start | bytes 4456448 | tf_op jit(solution)/shard_map/all_gather | solution.py:22
  51.0 3.1 %copy-start.3 = (bf16[64,8,8,128]{3,2,1,0:T(8,128)(2,1)}, bf16[64,8,8,128]{3,2,1,0:T(8,128)(2,1)S(1)}, u32[]{:S(2)}) copy-start(bf16[64,8,8,128]{3,2,1,0:T(8,128)(2,1)S(1)} %copy.54) | copy-start | bytes 3145732
  55.4 1.9 copy-start
  106.6 3.6 %copy-start.4 = (bf16[64,8,8,128]{3,2,1,0:T(8,128)(2,1)S(1)}, bf16[64,8,8,128]{3,2,1,0:T(8,128)(2,1)}, u32[]{:S(2)}) copy-start(bf16[64,8,8,128]{3,2,1,0:T(8,128)(2,1)} %copy-done.3) | copy-start | bytes 3145732
  109.2 1.0 copy-start.1
  111.6 133.3 %reduce-scatter.2.cloned.1.call-start = ((), (), s32[]{:S(2)}) async-start(), calls=%async_computation.2 | async-start | bytes 4456448 | tf_op jit(solution)/shard_map/reduce_scatter | solution.py:120
  150.6 1.9 copy-start.6
  156.8 88.0 %copy-start.7 = (f32[128,1024]{1,0:T(8,128)S(1)}, f32[128,1024]{1,0:T(8,128)}, u32[]{:S(2)}) copy-start(f32[128,1024]{1,0:T(8,128)} %param.16) | copy-start | bytes 1572868
  156.9 109.8 %copy-start.8 = (f32[128,1024]{1,0:T(8,128)S(1)}, f32[128,1024]{1,0:T(8,128)}, u32[]{:S(2)}) copy-start(f32[128,1024]{1,0:T(8,128)} %param.17) | copy-start | bytes 1572868
  246.0 6.5 %collective-permute-start = (bf16[128,1024]{1,0:T(8,128)(2,1)S(1)}, bf16[128,1024]{1,0:T(8,128)(2,1)S(1)}, u32[]{:S(2)}, u32[]{:S(2)}) collective-permute-start(bf16[128,1024]{1,0:T(8,128)(2,1)S(1)} %get-tuple-element.115), channel_id=1, source_target_pairs={{0,2},{2,0},{4,6},{6,4},{8,10},{10,8},{12,14},{14,12},{1,3},{3,1},... | collective-permute-start | bytes 786440 | tf_op jit(solution)/shard_map/ppermute | solution.py:39
  252.6 14.1 %collective-permute-start.1 = (bf16[128,1024]{1,0:T(8,128)(2,1)S(1)}, bf16[128,1024]{1,0:T(8,128)(2,1)S(1)}, u32[]{:S(2)}, u32[]{:S(2)}) collective-permute-start(bf16[128,1024]{1,0:T(8,128)(2,1)S(1)} %fusion.17), channel_id=1, source_target_pairs={{0,4},{4,0},{2,6},{6,2},{8,12},{12,8},{10,14},{14,10},{1,5},{5,1},... | collective-permute-start | bytes 786440 | tf_op jit(solution)/shard_map/ppermute | solution.py:39
Sparse Core Ops, SparseCore 0:
  49.6 40.5 all-gather.4
  111.7 38.7 all-gather.6
  157.0 87.8 reduce-scatter.1
